TPU v7x, 32 devices: a whole 2x2x4 slice. The times are simulated.
32 devices in a mesh: seq: 16 (over z, y, core), dp: 2 (over x).
Axes of the slice: x: 2, y: 2, z: 4, core: 2. Of those that a mesh axis runs over, the one named last changes fastest.
Arguments:
- layer_input: bfloat16 [2, 2048, 4096], P('dp', 'seq'), may hold values from -0.3125 to 0.3125
- scan_input: bfloat16 [2, 2048, 2048], P('dp', 'seq'), may hold values from -6 to 6
- readout: bfloat16 [2, 2048, 64], P('dp', 'seq'), may hold values from -6 to 6
- log_decay: float32 [2, 2048, 32], P('dp', 'seq'), may hold values from -1 to 0
- output_cotangent: bfloat16 [2, 2048, 2048], P('dp', 'seq'), may hold values from -0.0078125 to 0.0078125
- write_weight: float32 [4096, 64], P('dp'), may hold values from -6 to 6
- first_moment: float32 [4096, 64], P('dp'), may hold values from -6 to 6
- second_moment: float32 [4096, 64], P('dp'), may hold values from 1 to 25
Outputs:
- decay_gradient: float32 [2, 2048, 32], P('dp', 'seq')
- new_weight: float32 [4096, 64], P('dp')
- new_first: float32 [4096, 64], P('dp')
- new_second: float32 [4096, 64], P('dp')
All inputs are finite; a program needn't handle non-finite values.
Results may differ from a plain program's by a relative error of at most 0.0039.
Values may be sent and summed in bfloat16 or wider, within the bound.
A program may use at most 64 MiB of HBM per device.

v0:
```python
import jax
import jax.numpy as jnp
from jax import lax
from jax.sharding import PartitionSpec as P

HALF_HEAD_COUNT = 32
HEAD_DIM = 64
STATE = 64
beta_one = 0.9
beta_two = 0.999
adam_count = 10.0
learn_rate = 0.01
weight_decay = 0.1
epsilon = 1e-08
highest = lax.Precision.HIGHEST


def entering(part, axis, combine, identity, reverse):
    count = lax.axis_size(axis)
    place = lax.axis_index(axis)
    ahead = count - 1 - place if reverse else place
    gathered = jax.tree.map(lambda a: lax.all_gather(a, axis), part)
    state = jax.tree.map(lambda a, e: jnp.zeros_like(a) + jnp.asarray(e, a.dtype), part, identity)

    def one(lap, state):
        source = count - 1 - lap if reverse else lap
        return combine(
            state, jax.tree.map(lambda a: lax.dynamic_index_in_dim(a, source, 0, False), gathered)
        )

    return lax.fori_loop(0, ahead, one, state)


def pair_combine(earlier_pair, later_pair):
    return (
        earlier_pair[0] * later_pair[0],
        later_pair[0][:, None, None] * earlier_pair[1] + later_pair[1],
    )


def adam_update(grad_rows, weight_rows, first_rows, second_rows):
    new_first = beta_one * first_rows + (1.0 - beta_one) * grad_rows
    new_second = beta_two * second_rows + (1.0 - beta_two) * grad_rows * grad_rows
    first_hat = new_first / (1.0 - beta_one**adam_count)
    second_hat = new_second / (1.0 - beta_two**adam_count)
    new_weight = weight_rows - learn_rate * (
        first_hat / (jnp.sqrt(second_hat) + epsilon) + weight_decay * weight_rows
    )
    return (new_weight, new_first, new_second)


def on_device(
    layer_input,
    scan_input,
    readout,
    log_decay,
    output_cotangent,
    write_weight,
    first_moment,
    second_moment,
):
    input_rows = layer_input[0]
    scan_rows = scan_input[0]
    read_rows = readout[0]
    decay_rows = log_decay[0]
    back_rows = output_cotangent[0]
    length = input_rows.shape[0]
    weight_half = write_weight.astype(jnp.bfloat16)
    write_sum = jnp.dot(
        input_rows,
        lax.all_gather(weight_half, "dp", axis=0, tiled=True),
        preferred_element_type=jnp.float32,
    )
    write_half = write_sum.astype(jnp.bfloat16)
    write_float = lax.optimization_barrier(write_half).astype(jnp.float32)
    running = jnp.cumsum(decay_rows, axis=0)
    overall = running[-1]
    to_end = jnp.exp(overall[None, :] - running)
    from_start = jnp.exp(running)
    scan_split = scan_rows.reshape(length, HALF_HEAD_COUNT, HEAD_DIM)
    back_split = back_rows.reshape(length, HALF_HEAD_COUNT, HEAD_DIM)
    scan_heads = scan_split.astype(jnp.float32)
    back_heads = back_split.astype(jnp.float32)
    read_float = read_rows.astype(jnp.float32)
    state_local = jnp.einsum(
        "shp,sn->hpn", scan_heads * to_end[:, :, None], write_float, precision=highest
    )
    reverse_local = jnp.einsum(
        "shp,sn->hpn", back_heads * from_start[:, :, None], read_float, precision=highest
    )
    decay_total = jnp.exp(overall)
    identity = (
        jnp.ones((HALF_HEAD_COUNT,), jnp.float32),
        jnp.zeros((HALF_HEAD_COUNT, HEAD_DIM, STATE), jnp.float32),
    )
    state_pair = entering((decay_total, state_local), "seq", pair_combine, identity, False)
    grad_pair = entering((decay_total, reverse_local), "seq", pair_combine, identity, True)
    state_before = state_pair[1]
    grad_after = grad_pair[1]
    term_one = decay_total * jnp.sum(grad_after * state_before, axis=(1, 2))
    grad_write = jnp.einsum("hpn,sn->shp", grad_after, write_float, precision=highest)
    second_rows = to_end * jnp.sum(scan_heads * grad_write, axis=2)
    term_two = jnp.cumsum(second_rows, axis=0) - second_rows
    state_read = jnp.einsum("hpn,sn->shp", state_before, read_float, precision=highest)
    third_rows = from_start * jnp.sum(back_heads * state_read, axis=2)
    term_three = jnp.flip(jnp.cumsum(jnp.flip(third_rows, 0), axis=0), 0)
    crossed = jnp.einsum("thp,shp->hts", scan_split, back_split, preferred_element_type=jnp.float32)
    heads_running = running.T
    spread = heads_running[:, None, :] - heads_running[:, :, None]
    row_index = lax.broadcasted_iota(jnp.int32, (length, length), 0)
    col_index = lax.broadcasted_iota(jnp.int32, (length, length), 1)
    kernel_mat = (
        jnp.where((row_index <= col_index)[None], jnp.exp(jnp.minimum(spread, 0.0)), 0.0) * crossed
    )
    write_read = jnp.dot(write_half, read_rows.T, preferred_element_type=jnp.float32)
    pairing = jnp.where((row_index < col_index)[None], kernel_mat * write_read[None], 0.0)
    balance = (jnp.sum(pairing, axis=2) - jnp.sum(pairing, axis=1)).T
    term_four = jnp.cumsum(balance, axis=0) - balance
    decay_grad = term_one[None, :] + term_two + term_three + term_four
    scaled_scan = (scan_heads * to_end[:, :, None]).reshape(length, HALF_HEAD_COUNT * HEAD_DIM)
    write_grad = jnp.dot(
        scaled_scan, grad_after.reshape(HALF_HEAD_COUNT * HEAD_DIM, STATE), precision=highest
    )
    write_grad = write_grad + jnp.dot(jnp.sum(kernel_mat, axis=0), read_float, precision=highest)
    grad_half = write_grad.astype(jnp.bfloat16)
    partial_grad = jnp.dot(input_rows.T, grad_half, preferred_element_type=jnp.float32)
    owner_grad = lax.psum_scatter(partial_grad, "dp", scatter_dimension=0, tiled=True)
    grad_rows = lax.psum(owner_grad, "seq")
    new_weight, new_first, new_second = adam_update(
        grad_rows, write_weight, first_moment, second_moment
    )
    return (decay_grad[None], new_weight, new_first, new_second)


def solution(mesh):
    in_specs = (
        P("dp", "seq", None),
        P("dp", "seq", None),
        P("dp", "seq", None),
        P("dp", "seq", None),
        P("dp", "seq", None),
        P("dp", None),
        P("dp", None),
        P("dp", None),
    )
    out_specs = (P("dp", "seq", None), P("dp", None), P("dp", None), P("dp", None))
    return jax.shard_map(
        on_device, mesh=mesh, in_specs=in_specs, out_specs=out_specs, check_vma=False
    )
```

profile of v0, /device:TPU:29, one launch (start us, length us, event | category | flops | bytes accessed | tf_op | source)
XLA Modules:
  0.0 436.1 jit_solution(12412782208266294412)
XLA Ops:
  7.2 0.0 all-gather.6.cloned.1.call-start
  7.2 0.9 copy.43
  8.1 0.2 reduce_window_sum.22
  8.3 0.1 copy.45
  8.4 1.3 copy.44
  9.7 0.1 bitcast_multiply_fusion
  9.8 1.6 fusion.17
  11.4 0.0 all-gather.6.cloned.1.call-update
  11.5 0.0 reduce-scatter.2.cloned.1.call-start
  11.5 0.1 copy.47
  11.6 0.3 copy.46
  11.9 7.8 %all_gather.24 = bf16[4096,64]{0,1:T(8,128)(2,1)S(1)} all-gather(bf16[2048,64]{0,1:T(8,128)(2,1)S(1)} %convert_element_type.22), channel_id=1, replica_groups=mesh['seq'=16,'dp'=2] {'dp'}, dimensions={0}, use_global_device_ids=true | all-gather | bytes 786432 | tf_op jit(solution)/shard_map/all_gather | solution.py:71
  19.8 0.5 convolution_convert_fusion
  20.3 0.1 copy.53
  20.3 18.4 %all-gather.2 = f32[16,1,32]{2,1,0:T(1,128)S(1)} all-gather(f32[1,1,32]{2,1,0:T(1,128)S(1)} %get-tuple-element.175), channel_id=1, replica_groups=mesh['seq'=16,'dp'=2] {'seq'}, dimensions={0}, use_global_device_ids=true | all-gather | bytes 2176 | tf_op jit(solution)/shard_map/all_gather | solution.py:22
  38.7 0.2 fusion.20
  38.9 1.8 fusion
  40.8 95.8 %all-gather.6.cloned.1.call-done = f32[512,64,64]{2,1,0:T(8,128)} async-done(((f32[32,64,64]{2,1,0:T(8,128)}), f32[512,64,64]{2,1,0:T(8,128)}) %all-gather.6.cloned.1.call-update) | async-done | bytes 8388624 | tf_op jit(solution)/shard_map/all_gather | solution.py:22
  136.6 0.1 broadcast_in_dim.36.clone
  136.7 0.6 fusion.5
  137.3 0.1 fusion.25
  137.4 1.9 fusion.7
  139.3 0.2 fusion.8
  139.5 1.3 convolution_bitcast_fusion
  140.8 0.0 reduce-scatter.2.cloned.1.call-update
  140.8 0.0 all-reduce.2.cloned.1.call-start
  140.9 42.5 %reduce-scatter.2.cloned.1.call-done = f32[2048,64]{0,1:T(8,128)} async-done(((f32[4096,64]{0,1:T(8,128)}), f32[2048,64]{0,1:T(8,128)}) %reduce-scatter.2.cloned.1.call-update) | async-done | bytes 524304 | tf_op jit(solution)/shard_map/reduce_scatter | solution.py:127
  183.4 0.0 all-gather.8.cloned.1.call-start
  183.4 1.6 fusion.4
  185.1 0.0 all-gather.8.cloned.1.call-update
  185.1 0.1 copy.55
  185.2 0.2 reduce_window_sum.32
  185.4 0.1 copy.56
  185.4 0.1 copy.48
  185.5 0.2 reduce_window_sum.23
  185.7 0.1 copy.49
  185.8 90.6 %all-reduce.2.cloned.1.call-done = f32[2048,64]{0,1:T(8,128)} async-done(((f32[2048,64]{0,1:T(8,128)}), f32[2048,64]{0,1:T(8,128)}) %all-reduce.2.cloned.1.call-update) | async-done | bytes 524304 | tf_op jit(solution)/shard_map/psum | solution.py:128
  276.4 2.7 multiply_subtract_fusion
  279.2 125.0 %all-gather.8.cloned.1.call-done = f32[512,64,64]{2,1,0:T(8,128)} async-done(((f32[32,64,64]{2,1,0:T(8,128)}), f32[512,64,64]{2,1,0:T(8,128)}) %all-gather.8.cloned.1.call-update) | async-done | bytes 8388624 | tf_op jit(solution)/shard_map/all_gather | solution.py:22
  404.2 0.1 broadcast_in_dim.36
  404.3 22.4 %while.27 = (s32[]{:T(128)}, f32[32,64,64]{2,1,0:T(8,128)S(1)}, s32[]{:T(128)}, f32[16,32]{1,0:T(8,128)S(1)}, f32[16,32,64,64]{3,2,1,0:T(8,128)}, /*index=5*/s32[]{:T(128)}, s32[]{:T(128)}, s32[]{:T(128)}) while((s32[]{:T(128)}, f32[32,64,64]{2,1,0:T(8,128)S(1)}, s32[]{:T(128)}, f32[16,32]{1,0:T(8,128)S(1)}, f32[16,32,64,64]{3,2,1,0:T(8,128)}, ...), condition=%wide.region_4.5_spmd, body=%wide.region_3.4_spmd.sunk | while | flops 262149 | bytes 1573375 | solution.py:31
  404.3 1.4 bitcast_add_fusion.5
  405.8 1.4 bitcast_add_fusion.5
  407.3 1.4 bitcast_add_fusion.5
  408.8 1.4 bitcast_add_fusion.5
  410.3 1.4 bitcast_add_fusion.5
  411.8 1.4 bitcast_add_fusion.5
  413.3 1.4 bitcast_add_fusion.5
  414.8 1.4 bitcast_add_fusion.5
  416.3 1.4 bitcast_add_fusion.5
  417.8 1.4 bitcast_add_fusion.5
  419.3 1.4 bitcast_add_fusion.5
  420.8 1.4 bitcast_add_fusion.5
  422.3 1.4 bitcast_add_fusion.5
  423.8 1.4 bitcast_add_fusion.5
  425.3 1.4 bitcast_add_fusion.5
  426.8 0.3 multiply_reduce_fusion
  427.1 0.7 copy-done.2
  427.8 0.6 fusion.6
  428.5 0.1 copy.51
  428.6 0.2 reduce_window_sum.27
  428.8 0.1 copy.52
  428.8 0.1 rev.8
  428.9 0.7 add_bitcast_fusion
  (36 shorter events, 0.3 us)
Async XLA Ops:
  7.2 12.6 %copy-start = (bf16[1,128,4096]{2,1,0:T(8,128)(2,1)S(1)}, bf16[1,128,4096]{2,1,0:T(8,128)(2,1)}, u32[]{:S(2)}) copy-start(bf16[1,128,4096]{2,1,0:T(8,128)(2,1)} %param.12) | copy-start | bytes 3145732
  7.2 2.6 copy-start.5
  7.2 129.4 %all-gather.6.cloned.1.call-start = ((), (), s32[]{:S(2)}) async-start(), calls=%async_computation.3 | async-start | bytes 17825792 | tf_op jit(solution)/shard_map/all_gather | solution.py:22
  9.7 29.2 %copy-start.1 = (bf16[1,128,2048]{1,2,0:T(8,128)(2,1)}, bf16[1,128,2048]{1,2,0:T(8,128)(2,1)S(1)}, u32[]{:S(2)}) copy-start(bf16[1,128,2048]{1,2,0:T(8,128)(2,1)S(1)} %copy.44) | copy-start | bytes 1572868
  9.7 1.9 copy-start.4
  9.8 2.0 copy-start.3
  11.5 171.9 %reduce-scatter.2.cloned.1.call-start = ((), (), s32[]{:S(2)}) async-start(), calls=%async_computation.1 | async-start | bytes 1572864 | tf_op jit(solution)/shard_map/reduce_scatter | solution.py:127
  140.8 135.6 %all-reduce.2.cloned.1.call-start = ((), (), s32[]{:S(2)}) async-start(), calls=%async_computation.2 | async-start | bytes 1048576 | tf_op jit(solution)/shard_map/psum | solution.py:128
  183.4 220.8 %all-gather.8.cloned.1.call-start = ((), (), s32[]{:S(2)}) async-start(), calls=%async_computation.4 | async-start | bytes 17825792 | tf_op jit(solution)/shard_map/all_gather | solution.py:22
  426.8 1.0 copy-start.2
Sparse Core Ops, SparseCore 0:
  11.6 124.9 all-gather.5
  140.9 42.3 reduce-scatter.1
  186.8 89.6 all-reduce.1
  278.4 125.7 all-gather.7
where the time goes:
time: 437 us; the launch traced here: 436 us
  waiting for transfers between devices  354 us (81%)
  other arithmetic  26.4 us (6%)
  blocking collectives  26.2 us (6%)
  between operations  14 us (3%)
  matrix products  10.4 us (2%)
    all_gather x2, waiting for transfers between devices, entering(): gathered = jax.tree.map(lambda a: lax.all_gather(a, axis), part)  221 us
    psum x1, waiting for transfers between devices, on_device(): grad_rows = lax.psum(owner_grad, 'seq')  90.6 us
    reduce_scatter x1, waiting for transfers between devices, on_device(): lax.psum_scatter(partial_grad, 'dp', scatter_dimension=0, tiled=True)  42.5 us
    add x15, other arithmetic, pair_combine(): later_pair[0][:, None, None] * earlier_pair[1] + later_pair[1]  21.7 us
    all_gather x1, blocking collectives, entering(): gathered = jax.tree.map(lambda a: lax.all_gather(a, axis), part)  18.4 us
  transfers between devices with their start and end apart: 4, of which 4 were waited for; matrix products, arithmetic and copies ran while one was open for 2% of the time, Pallas kernels for 0%

commit v1 on v0

--- a/solution.py
+++ b/solution.py
@@ -125,7 +125,7 @@
     grad_half = write_grad.astype(jnp.bfloat16)
     partial_grad = jnp.dot(input_rows.T, grad_half, preferred_element_type=jnp.float32)
     owner_grad = lax.psum_scatter(partial_grad, "dp", scatter_dimension=0, tiled=True)
-    grad_rows = lax.psum(owner_grad, "seq")
+    grad_rows = jnp.sum(lax.all_gather(owner_grad, "seq"), axis=0)
     new_weight, new_first, new_second = adam_update(
         grad_rows, write_weight, first_moment, second_moment
     )

time: 437 us -> 407 us (0.931)
  waiting for transfers between devices: 354 us -> 311 us
  local copies, waits for them, and re-layouts: 4.35 us -> 11.8 us
    psum x1 -> x0, waiting for transfers between devices: 90.6 us -> none  [on_device(): grad_rows = lax.psum(owner_grad, 'seq')]
    all_gather x0 -> x1, waiting for transfers between devices: none -> 49 us  [on_device(): grad_rows = jnp.sum(lax.all_gather(owner_grad, 'seq'), axis=0)]
    unnamed x14 -> x19, local copies, waits for them, and re-layouts: 2.36 us -> 9.79 us
  transfers between devices with their start and end apart: 4 -> 4, of which waited for: 4 -> 4; matrix products, arithmetic and copies ran while one was open for 2% -> 8% of each run, Pallas kernels for 0% -> 0%
where the time goes in v1:
time: 407 us; the launch traced here: 403 us
  waiting for transfers between devices  311 us (76%)
  other arithmetic  26.9 us (7%)
  blocking collectives  26.2 us (6%)
  between operations  14.1 us (3%)
  local copies, waits for them, and re-layouts  11.8 us (3%)
  matrix products  11.5 us (3%)
    all_gather x2, waiting for transfers between devices, entering(): gathered = jax.tree.map(lambda a: lax.all_gather(a, axis), part)  221 us
    all_gather x1, waiting for transfers between devices, on_device(): grad_rows = jnp.sum(lax.all_gather(owner_grad, 'seq'), axis=0)  49 us
    reduce_scatter x1, waiting for transfers between devices, on_device(): lax.psum_scatter(partial_grad, 'dp', scatter_dimension=0, tiled=True)  40.7 us
    add x15, other arithmetic, pair_combine(): later_pair[0][:, None, None] * earlier_pair[1] + later_pair[1]  21.8 us
    all_gather x1, blocking collectives, entering(): gathered = jax.tree.map(lambda a: lax.all_gather(a, axis), part)  18.4 us
    unnamed x19, local copies, waits for them, and re-layouts  9.79 us
  transfers between devices with their start and end apart: 4, of which 4 were waited for; matrix products, arithmetic and copies ran while one was open for 8% of the time, Pallas kernels for 0%

profile of v1, /device:TPU:29, one launch (start us, length us, event | category | flops | bytes accessed | tf_op | source)
XLA Modules:
  0.0 402.6 jit_solution(10034673811869322434)
XLA Ops:
  7.2 0.0 all-gather.8.cloned.1.call-start
  7.2 0.9 copy.43
  8.1 0.2 reduce_window_sum.22
  8.3 0.1 copy.45
  8.4 1.3 copy.44
  9.7 0.1 bitcast_multiply_fusion
  9.8 1.6 fusion.17
  11.4 0.0 all-gather.8.cloned.1.call-update
  11.5 0.0 reduce-scatter.2.cloned.1.call-start
  11.5 0.1 copy.47
  11.6 0.3 copy.46
  11.9 7.8 %all_gather.30 = bf16[4096,64]{0,1:T(8,128)(2,1)S(1)} all-gather(bf16[2048,64]{0,1:T(8,128)(2,1)S(1)} %convert_element_type.22), channel_id=1, replica_groups=mesh['seq'=16,'dp'=2] {'dp'}, dimensions={0}, use_global_device_ids=true | all-gather | bytes 786432 | tf_op jit(solution)/shard_map/all_gather | solution.py:71
  19.8 0.5 convolution_convert_fusion
  20.3 0.1 copy.53
  20.3 18.4 %all-gather.3 = f32[16,1,32]{2,1,0:T(1,128)S(1)} all-gather(f32[1,1,32]{2,1,0:T(1,128)S(1)} %get-tuple-element.175), channel_id=1, replica_groups=mesh['seq'=16,'dp'=2] {'seq'}, dimensions={0}, use_global_device_ids=true | all-gather | bytes 2176 | tf_op jit(solution)/shard_map/all_gather | solution.py:22
  38.7 0.2 fusion.20
  38.9 1.8 fusion
  40.8 95.8 %all-gather.8.cloned.1.call-done = f32[512,64,64]{2,1,0:T(8,128)} async-done(((f32[32,64,64]{2,1,0:T(8,128)}), f32[512,64,64]{2,1,0:T(8,128)}) %all-gather.8.cloned.1.call-update) | async-done | bytes 8388624 | tf_op jit(solution)/shard_map/all_gather | solution.py:22
  136.6 0.1 broadcast_in_dim.36.clone
  136.7 0.6 fusion.5
  137.3 0.1 fusion.25
  137.4 1.9 fusion.7
  139.3 0.2 fusion.8
  139.5 1.3 convolution_bitcast_fusion
  140.8 0.0 reduce-scatter.2.cloned.1.call-update
  140.8 0.0 all-gather.10.cloned.1.call-start
  140.9 1.7 fusion.4
  142.6 0.0 all-gather.12.cloned.1.call-start
  142.7 40.7 %reduce-scatter.2.cloned.1.call-done = f32[2048,64]{0,1:T(8,128)} async-done(((f32[4096,64]{0,1:T(8,128)}), f32[2048,64]{0,1:T(8,128)}) %reduce-scatter.2.cloned.1.call-update) | async-done | bytes 524304 | tf_op jit(solution)/shard_map/reduce_scatter | solution.py:127
  183.4 0.1 copy.55
  183.5 0.2 reduce_window_sum.32
  183.7 0.1 copy.56
  183.7 0.1 copy.48
  183.8 0.2 reduce_window_sum.23
  184.0 0.1 copy.49
  184.1 125.6 %all-gather.10.cloned.1.call-done = f32[512,64,64]{2,1,0:T(8,128)} async-done(((f32[32,64,64]{2,1,0:T(8,128)}), f32[512,64,64]{2,1,0:T(8,128)}) %all-gather.10.cloned.1.call-update) | async-done | bytes 8388624 | tf_op jit(solution)/shard_map/all_gather | solution.py:22
  309.7 0.1 broadcast_in_dim.36
  309.8 22.8 %while.27 = (s32[]{:T(128)}, f32[32,64,64]{2,1,0:T(8,128)S(1)}, s32[]{:T(128)}, f32[16,32]{1,0:T(8,128)S(1)}, f32[16,32,64,64]{3,2,1,0:T(8,128)}, /*index=5*/s32[]{:T(128)}, s32[]{:T(128)}, s32[]{:T(128)}) while((s32[]{:T(128)}, f32[32,64,64]{2,1,0:T(8,128)S(1)}, s32[]{:T(128)}, f32[16,32]{1,0:T(8,128)S(1)}, f32[16,32,64,64]{3,2,1,0:T(8,128)}, ...), condition=%wide.region_4.5_spmd, body=%wide.region_3.4_spmd.sunk | while | flops 262149 | bytes 1573375 | solution.py:31
  309.9 1.4 bitcast_add_fusion.5
  311.4 1.4 bitcast_add_fusion.5
  312.9 1.4 bitcast_add_fusion.5
  314.3 1.4 bitcast_add_fusion.5
  315.8 1.4 bitcast_add_fusion.5
  317.3 1.4 bitcast_add_fusion.5
  318.8 1.5 bitcast_add_fusion.5
  320.3 1.5 bitcast_add_fusion.5
  321.9 1.5 bitcast_add_fusion.5
  323.4 1.4 bitcast_add_fusion.5
  324.9 1.5 bitcast_add_fusion.5
  326.4 1.4 bitcast_add_fusion.5
  327.9 1.5 bitcast_add_fusion.5
  329.4 1.4 bitcast_add_fusion.5
  330.9 1.4 bitcast_add_fusion.5
  332.6 1.7 fusion.6
  334.3 0.1 copy.51
  334.4 0.2 reduce_window_sum.27
  334.6 0.1 copy.52
  334.6 0.1 rev.8
  334.7 0.3 multiply_reduce_fusion
  335.1 0.7 add_bitcast_fusion
  335.8 49.0 %all-gather.12.cloned.1.call-done = f32[32768,64]{0,1:T(8,128)} async-done(((f32[2048,64]{0,1:T(8,128)}), f32[32768,64]{0,1:T(8,128)}) %all-gather.12.cloned.1.call-update) | async-done | bytes 8388624 | tf_op jit(solution)/shard_map/all_gather | solution.py:128
  384.8 8.1 %copy.59 = f32[8,8,16,2048]{3,2,1,0:T(8,128)S(1)} copy(f32[8,8,16,2048]{3,1,2,0:T(8,128)} %bitcast.89) | data formatting | bytes 16777216
  393.0 1.7 bitcast_reduce_fusion
  394.7 1.4 multiply_subtract_fusion
  (42 shorter events, 0.4 us)
Async XLA Ops:
  7.2 12.6 %copy-start = (bf16[1,128,4096]{2,1,0:T(8,128)(2,1)S(1)}, bf16[1,128,4096]{2,1,0:T(8,128)(2,1)}, u32[]{:S(2)}) copy-start(bf16[1,128,4096]{2,1,0:T(8,128)(2,1)} %param.12) | copy-start | bytes 3145732
  7.2 2.6 copy-start.7
  7.2 129.4 %all-gather.8.cloned.1.call-start = ((), (), s32[]{:S(2)}) async-start(), calls=%async_computation.2 | async-start | bytes 17825792 | tf_op jit(solution)/shard_map/all_gather | solution.py:22
  9.7 29.2 %copy-start.1 = (bf16[1,128,2048]{1,2,0:T(8,128)(2,1)}, bf16[1,128,2048]{1,2,0:T(8,128)(2,1)S(1)}, u32[]{:S(2)}) copy-start(bf16[1,128,2048]{1,2,0:T(8,128)(2,1)S(1)} %copy.44) | copy-start | bytes 1572868
  9.7 1.9 copy-start.6
  9.8 2.0 copy-start.2
  11.5 171.9 %reduce-scatter.2.cloned.1.call-start = ((), (), s32[]{:S(2)}) async-start(), calls=%async_computation.1 | async-start | bytes 1572864 | tf_op jit(solution)/shard_map/reduce_scatter | solution.py:127
  140.8 168.9 %all-gather.10.cloned.1.call-start = ((), (), s32[]{:S(2)}) async-start(), calls=%async_computation.3 | async-start | bytes 17825792 | tf_op jit(solution)/shard_map/all_gather | solution.py:22
  142.6 242.2 %all-gather.12.cloned.1.call-start = ((), (), s32[]{:S(2)}) async-start(), calls=%async_computation.4 | async-start | bytes 8912896 | tf_op jit(solution)/shard_map/all_gather | solution.py:128
  392.9 1.8 copy-start.3
  392.9 1.8 copy-start.4
  392.9 1.8 copy-start.5
Sparse Core Ops, SparseCore 0:
  11.6 124.9 all-gather.7
  141.0 42.3 reduce-scatter.1
  185.5 124.1 all-gather.9
  311.7 73.0 all-gather.11
